TPU v7x, 32 devices: a whole 2x2x4 slice. The times are simulated.
32 devices in a mesh: groups: 2 (over y), wide: 8 (over z, x), narrow: 2 (over core).
Axes of the slice: x: 2, y: 2, z: 4, core: 2. Of those that a mesh axis runs over, the one named last changes fastest.
Arguments:
- goals: float32 [8192, 1024], P(('groups', 'wide', 'narrow')), parts along dimension 0, may hold values from -32 to 32
- premises: float32 [1024, 1024], P(('groups', 'wide', 'narrow')), parts along dimension 0, may hold values from -24 to 24
- counts: int32 [8192], P(('groups', 'wide')), parts along dimension 0, may hold values from 1 to 16
- positives: int32 [8192, 16], P(('groups', 'wide')), parts along dimension 0, may hold values from -1 to 511, as said below
- cotangent: float32 [8192], P(('groups', 'wide')), parts along dimension 0, may hold values from -6 to 6
Outputs:
- goal_loss: float32 [8192], P(('groups', 'wide')), parts along dimension 0
- grad_goals: float32 [8192, 1024], P(('groups', 'wide', 'narrow')), parts along dimension 0
- grad_premises: float32 [1024, 1024], P(('groups', 'wide', 'narrow')), parts along dimension 0
There are 2 independent parts, one for each index of `groups`. A program takes and returns all parts, laid end to end along the dimension named above; each array names one. Nothing has to cross between parts.
Inputs may be any that keep to these rules, and one draw needn't show every extreme that they name: positives[i, k] is a premise index for k < counts[i] and -1 from there on.
All inputs are finite; a program needn't handle non-finite values.
Results may differ from a plain program's by a relative error of at most 0.012.
The roundings to bfloat16 on the way count: a program that leaves them out, or rounds other values in their place, can miss the bound.
Values may be sent and summed in bfloat16 or wider, within the bound.
A program may use at most 64 MiB of HBM per device.

v0:
```python
import jax
import jax.numpy as jnp
from jax import lax
from jax.sharding import PartitionSpec as P


def hit_counts(row_lists, column_ids):
    total = jnp.zeros((row_lists.shape[0], column_ids.shape[0]), jnp.float32)
    for which_slot in range(row_lists.shape[1]):
        total = total + (row_lists[:, which_slot][:, None] == column_ids[None, :]).astype(
            jnp.float32
        )
    return total


def per_device(goals, premises, counts, positives, cotangent):
    goal_part = goals.astype(jnp.bfloat16)
    prem_part = premises.astype(jnp.bfloat16)
    prem_rows = prem_part.shape[0]
    width = goal_part.shape[1]
    scale = width ** (-0.5)
    n_wide = lax.axis_size("wide")
    n_narrow = lax.axis_size("narrow")
    narrow_index = lax.axis_index("narrow")
    rows_block = lax.all_gather(goal_part, "narrow", axis=0, tiled=True)
    prem_block = lax.all_gather(prem_part, "wide", axis=0, tiled=True)
    goal_counts = counts.astype(jnp.float32)
    local_ids = jnp.arange(prem_rows * n_wide, dtype=jnp.int32)
    column_ids = (
        local_ids // prem_rows * n_narrow + narrow_index
    ) * prem_rows + local_ids % prem_rows
    col_total = prem_block.shape[0]
    row_total = rows_block.shape[0]
    step_cols = 512 if col_total % 512 == 0 else col_total
    starts = list(range(0, col_total, step_cols))

    def tile_scores(begin):
        piece = prem_block[begin : begin + step_cols]
        return (
            lax.dot_general(
                rows_block, piece, (((1,), (1,)), ((), ())), preferred_element_type=jnp.float32
            )
            * scale
        )

    top = jnp.full((row_total,), -jnp.inf, jnp.float32)
    total = jnp.zeros((row_total,), jnp.float32)
    positive_sum = jnp.zeros((row_total,), jnp.float32)
    for begin in starts:
        scores = tile_scores(begin)
        hits = hit_counts(positives, column_ids[begin : begin + step_cols])
        new_top = jnp.maximum(top, jnp.max(scores, axis=1))
        total = total * jnp.exp(top - new_top) + jnp.sum(jnp.exp(scores - new_top[:, None]), axis=1)
        positive_sum = positive_sum + jnp.sum(hits * scores, axis=1)
        top = new_top
    best = lax.pmax(top, "narrow")
    total_all, positive_all = lax.psum((total * jnp.exp(top - best), positive_sum), "narrow")
    log_total = best + jnp.log(total_all)
    row_loss = log_total - positive_all / goal_counts
    grad_rows = jnp.zeros((row_total, width), jnp.float32)
    pieces = []
    for number, begin in enumerate(starts):
        scores = tile_scores(begin)
        hits = hit_counts(positives, column_ids[begin : begin + step_cols])
        dscores = (
            cotangent[:, None]
            * (jnp.exp(scores - log_total[:, None]) - hits / goal_counts[:, None])
            * scale
        ).astype(jnp.bfloat16)
        grad_rows = grad_rows + jnp.dot(
            dscores, prem_block[begin : begin + step_cols], preferred_element_type=jnp.float32
        )
        pieces.append(dscores)
    stored = jnp.concatenate(pieces, axis=1)
    grad_goals = lax.psum_scatter(grad_rows, "narrow", scatter_dimension=0, tiled=True)
    grad_premises = lax.psum_scatter(
        lax.dot_general(
            stored, rows_block, (((0,), (0,)), ((), ())), preferred_element_type=jnp.float32
        ),
        "wide",
        scatter_dimension=0,
        tiled=True,
    )
    return (row_loss, grad_goals, grad_premises)


def solution(mesh):
    return jax.shard_map(
        per_device,
        mesh=mesh,
        in_specs=(
            P(("groups", "wide", "narrow"), None),
            P(("groups", "wide", "narrow"), None),
            P(("groups", "wide")),
            P(("groups", "wide"), None),
            P(("groups", "wide")),
        ),
        out_specs=(
            P(("groups", "wide")),
            P(("groups", "wide", "narrow"), None),
            P(("groups", "wide", "narrow"), None),
        ),
        check_vma=False,
    )
```

profile of v0, /device:TPU:0, one launch (start us, length us, event | category | flops | bytes accessed | tf_op | source)
XLA Modules:
  0.0 136.1 jit_solution(13301415830657365863)
XLA Ops:
  7.2 0.0 copy-start.2
  7.2 0.0 copy-start
  7.2 0.0 copy-start.1
  7.2 0.0 all-gather.2.cloned.1.call-start
  7.2 2.1 %convert_element_type.76 = bf16[256,1024]{1,0:T(8,128)(2,1)} convert(f32[256,1024]{1,0:T(8,128)} %param.5) | non-fusion elementwise | flops 262144 | bytes 1572864 | tf_op jit(solution)/shard_map/convert_element_type | solution.py:17
  9.4 0.0 copy-start.4
  9.4 0.0 all-gather.2.cloned.1.call-update
  9.4 0.0 reduce-scatter.5.cloned.1.call-start
  9.4 0.0 copy-done.2
  9.5 0.0 copy-done
  9.5 0.0 copy-done.1
  9.6 33.0 %all_gather.7 = bf16[256,1024]{1,0:T(8,128)(2,1)S(1)} all-gather(bf16[32,1024]{1,0:T(8,128)(2,1)S(1)} %convert_element_type.77), channel_id=1, replica_groups=mesh['groups'=2,'wide'=8,'narrow'=2] {'wide'}, dimensions={0}, use_global_device_ids=true | all-gather | bytes 589824 | tf_op jit(solution)/shard_map/all_gather | solution.py:26
  42.6 0.0 all-gather.2.cloned.1.call-done
  42.6 0.0 copy-start.3
  42.6 1.8 %fusion.9 = (f32[512]{0:T(512)S(1)}, f32[512,256]{0,1:T(8,128)S(1)}) fusion(bf16[512,1024]{1,0:T(8,128)(2,1)} %all-gather.2.cloned.1.call-done, bf16[256,1024]{1,0:T(8,128)(2,1)S(1)} %all_gather.7), kind=kOutput, calls=%fused_computation.22 | convolution fusion | flops 268697088 | bytes 2099200 | tf_op jit(solution)/shard_map/dot_general | solution.py:40
  44.4 2.5 %pmax.7 = f32[512]{0:T(512)S(1)} all-reduce(f32[512]{0:T(512)S(1)} %get-tuple-element.25), channel_id=1, replica_groups=mesh['groups'=2,'wide'=8,'narrow'=2] {'narrow'}, use_global_device_ids=true, to_apply=%region_1.2 | all-reduce | flops 512 | bytes 4096 | tf_op jit(solution)/shard_map/pmax | solution.py:56
  46.9 1.1 multiply_reduce_fusion
  47.9 2.5 %all-reduce = (f32[512]{0:T(512)S(1)}, f32[512]{0:T(512)S(1)}) all-reduce(f32[512]{0:T(512)S(1)} %exponential_multiply_fusion, f32[512]{0:T(512)S(1)} %get-tuple-element.3), channel_id=1, replica_groups=mesh['groups'=2,'wide'=8,'narrow'=2] {'narrow'}, use_global_device_ids=true, to_apply=%region_3.4 | all-reduce | flops 1024 | bytes 8192 | tf_op jit(solution)/shard_map/psum | solution.py:57
  50.4 0.6 divide_subtract_fusion
  51.0 0.0 copy-done.4
  51.0 0.0 copy-done.3
  51.0 2.3 %fusion.6 = f32[256,1024]{1,0:T(8,128)} fusion(bf16[512,1024]{1,0:T(8,128)(2,1)S(1)} %copy-done.3, f32[512,256]{0,1:T(8,128)S(1)} %get-tuple-element.26, f32[512]{0:T(512)S(1)} %convert_element_type.94, f32[512]{0:T(512)S(1)} %get-tuple-element.8, f32[512]{0:T(512)S(1)} %copy-done.4, s32[512]{0:T(512)S(1)} %bitcast.63, s32[512]{0:T(512)S(1)} %bitcast.66, ...), kind=kOutput, calls=%fused_computation.19 | convolution fusion | flops 275382272 | bytes 2661376 | tf_op jit(solution)/shard_map/dot_general | solution.py:77
  53.3 0.0 reduce-scatter.5.cloned.1.call-update
  53.3 0.0 reduce-scatter.3.cloned.1.call-start
  53.4 2.7 %fusion.7 = f32[512,1024]{1,0:T(8,128)} fusion(bf16[256,1024]{1,0:T(8,128)(2,1)S(1)} %all_gather.7, f32[512,256]{0,1:T(8,128)S(1)} %get-tuple-element.26, f32[512]{0:T(512)S(1)} %convert_element_type.94, f32[512]{0:T(512)S(1)} %get-tuple-element.8, f32[512]{0:T(512)S(1)} %copy-done.4, s32[512]{0:T(512)S(1)} %bitcast.64, s32[512]{0:T(512)S(1)} %bitcast.67, ...), kind=kOutput, calls=%fused_computation.20 | convolution fusion | flops 275382272 | bytes 3185664 | tf_op jit(solution)/shard_map/dot_general | solution.py:70
  56.1 0.0 reduce-scatter.3.cloned.1.call-update
  56.1 61.9 %reduce-scatter.5.cloned.1.call-done = f32[32,1024]{1,0:T(8,128)} async-done(((f32[256,1024]{1,0:T(8,128)}), f32[32,1024]{1,0:T(8,128)}) %reduce-scatter.5.cloned.1.call-update) | async-done | bytes 131088 | tf_op jit(solution)/shard_map/reduce_scatter | solution.py:76
  118.0 11.6 %reduce-scatter.3.cloned.1.call-done = f32[256,1024]{1,0:T(8,128)} async-done(((f32[512,1024]{1,0:T(8,128)}), f32[256,1024]{1,0:T(8,128)}) %reduce-scatter.3.cloned.1.call-update) | async-done | bytes 1048592 | tf_op jit(solution)/shard_map/reduce_scatter | solution.py:75
  (5 shorter events, 0.1 us)
Async XLA Ops:
  7.2 2.3 %copy-start.2 = (s32[512]{0:T(512)S(1)}, s32[512]{0:T(512)}, u32[]{:S(2)}) copy-start(s32[512]{0:T(512)} %param.7) | copy-start | bytes 6148
  7.2 2.3 %copy-start = (f32[32,1024]{1,0:T(8,128)S(1)}, f32[32,1024]{1,0:T(8,128)}, u32[]{:S(2)}) copy-start(f32[32,1024]{1,0:T(8,128)} %param.6) | copy-start | bytes 393220
  7.2 2.3 %copy-start.1 = (s32[512,16]{0,1:T(8,128)S(1)}, s32[512,16]{0,1:T(8,128)}, u32[]{:S(2)}) copy-start(s32[512,16]{0,1:T(8,128)} %param.8) | copy-start | bytes 98308
  7.2 35.4 %all-gather.2.cloned.1.call-start = ((), (), s32[]{:S(2)}) async-start(), calls=%async_computation.2 | async-start | bytes 1572864 | tf_op jit(solution)/shard_map/all_gather | solution.py:25
  9.4 41.6 %copy-start.4 = (f32[512]{0:T(512)S(1)}, f32[512]{0:T(512)}, u32[]{:S(2)}) copy-start(f32[512]{0:T(512)} %param.9) | copy-start | bytes 6148
  9.4 108.6 %reduce-scatter.5.cloned.1.call-start = ((), (), s32[]{:S(2)}) async-start(), calls=%async_computation.4 | async-start | bytes 1179648 | tf_op jit(solution)/shard_map/reduce_scatter | solution.py:76
  42.6 8.4 %copy-start.3 = (bf16[512,1024]{1,0:T(8,128)(2,1)S(1)}, bf16[512,1024]{1,0:T(8,128)(2,1)}, u32[]{:S(2)}) copy-start(bf16[512,1024]{1,0:T(8,128)(2,1)} %all-gather.2.cloned.1.call-done) | copy-start | bytes 3145732
  53.3 76.3 %reduce-scatter.3.cloned.1.call-start = ((), (), s32[]{:S(2)}) async-start(), calls=%async_computation.3 | async-start | bytes 3145728 | tf_op jit(solution)/shard_map/reduce_scatter | solution.py:75
Sparse Core Ops, SparseCore 0:
  10.1 11.7 all-gather.1
  53.4 64.5 reduce-scatter.4
  120.9 8.6 reduce-scatter.2
where the time goes:
time: 136 us
  waiting for transfers between devices  73.5 us (54%)
  blocking collectives  38 us (28%)
  between operations  13.8 us (10%)
  matrix products  6.82 us (5%)
  other arithmetic  3.82 us (3%)
    reduce_scatter x1, waiting for transfers between devices, per_device(): lax.psum_scatter(lax.dot_general(stored, rows_block, (((0,), (0,)), ((),...  61.9 us
    all_gather x1, blocking collectives, per_device(): prem_block = lax.all_gather(prem_part, 'wide', axis=0, tiled=True)  33 us
    reduce_scatter x1, waiting for transfers between devices, per_device(): lax.psum_scatter(grad_rows, 'narrow', scatter_dimension=0, tiled=True)  11.6 us
    dot_general x1, matrix products, per_device(): jnp.dot(dscores, prem_block[begin:begin + step_cols], preferred_element_t...  2.73 us
  transfers between devices with their start and end apart: 3, of which 2 were waited for; matrix products, arithmetic and copies ran while one was open for 2% of the time, Pallas kernels for 0%

commit v1 on v0

--- a/solution.py
+++ b/solution.py
@@ -1,7 +1,30 @@
+import functools
 import jax
 import jax.numpy as jnp
 from jax import lax
 from jax.sharding import PartitionSpec as P
+
+
+def clear_quarters_on(a0, dim_k):
+    a0 = jnp.moveaxis(a0, 0, dim_k)
+    local_now = a0.shape
+    return a0.reshape(
+        *local_now[:dim_k], local_now[dim_k] * local_now[dim_k + 1], *local_now[dim_k + 2 :]
+    )
+
+
+def sample_pack(unit, mesh_name, dim_i):
+    total_devices = lax.axis_size(mesh_name)
+    copies = tuple(((dev_i, (dev_i + 1) % total_devices) for dev_i in range(total_devices)))
+    all_blocks = [unit]
+    while len(all_blocks) < total_devices:
+        all_blocks.append(lax.ppermute(all_blocks[-1], axis_name=mesh_name, perm=copies))
+    z1 = lax.axis_index(mesh_name)
+    all_blocks = jnp.stack(all_blocks)[(z1 - jnp.arange(total_devices)) % total_devices]
+    return clear_quarters_on(all_blocks, dim_i)
+
+
+refer_flows_on = functools.partial(sample_pack, mesh_name="wide", dim_i=0)
 
 
 def hit_counts(row_lists, column_ids):
@@ -23,7 +46,7 @@
     n_narrow = lax.axis_size("narrow")
     narrow_index = lax.axis_index("narrow")
     rows_block = lax.all_gather(goal_part, "narrow", axis=0, tiled=True)
-    prem_block = lax.all_gather(prem_part, "wide", axis=0, tiled=True)
+    prem_block = refer_flows_on(prem_part)
     goal_counts = counts.astype(jnp.float32)
     local_ids = jnp.arange(prem_rows * n_wide, dtype=jnp.int32)
     column_ids = (

time: 136 us -> 151 us (1.11)
  waiting for transfers between devices: 73.5 us -> 117 us
  blocking collectives: 38 us -> 4.94 us
  starting transfers between devices: 0.12 us -> 3.13 us
    ppermute x0 -> x7, waiting for transfers between devices: none -> 47.3 us  [sample_pack(): lax.ppermute(all_blocks[-1], axis_name=mesh_name, perm=copies)]
    all_gather x1 -> x0, blocking collectives: 33 us -> none  [per_device(): prem_block = lax.all_gather(prem_part, 'wide', axis=0, tiled=True)]
    reduce_scatter x1, waiting for transfers between devices: 61.9 us -> 58.3 us  [per_device(): lax.psum_scatter(lax.dot_general(stored, rows_block, (((0,), (0,)), ((),...]
    ppermute x0 -> x7, starting transfers between devices: none -> 3.01 us  [sample_pack(): lax.ppermute(all_blocks[-1], axis_name=mesh_name, perm=copies)]
  transfers between devices with their start and end apart: 3 -> 10, of which waited for: 2 -> 9; matrix products, arithmetic and copies ran while one was open for 2% -> 2% of each run, Pallas kernels for 0% -> 0%
where the time goes in v1:
time: 151 us
  waiting for transfers between devices  117 us (77%)
  between operations  13.9 us (9%)
  matrix products  6.82 us (5%)
  blocking collectives  4.94 us (3%)
  other arithmetic  3.83 us (3%)
  starting transfers between devices  3.13 us (2%)
    reduce_scatter x1, waiting for transfers between devices, per_device(): lax.psum_scatter(lax.dot_general(stored, rows_block, (((0,), (0,)), ((),...  58.3 us
    ppermute x7, waiting for transfers between devices, sample_pack(): lax.ppermute(all_blocks[-1], axis_name=mesh_name, perm=copies)  47.3 us
    reduce_scatter x1, waiting for transfers between devices, per_device(): lax.psum_scatter(grad_rows, 'narrow', scatter_dimension=0, tiled=True)  11.6 us
  transfers between devices with their start and end apart: 10, of which 9 were waited for; matrix products, arithmetic and copies ran while one was open for 2% of the time, Pallas kernels for 0%

profile of v1, /device:TPU:0, one launch (start us, length us, event | category | flops | bytes accessed | tf_op | source)
XLA Modules:
  0.0 150.5 jit_solution(14446924091594846674)
XLA Ops:
  7.2 0.0 copy-start.1
  7.2 0.0 copy-start.3
  7.2 0.0 copy-start.2
  7.2 0.0 all-gather.2.cloned.1.call-start
  7.2 2.1 %convert_element_type.77 = bf16[256,1024]{1,0:T(8,128)(2,1)} convert(f32[256,1024]{1,0:T(8,128)} %param.5) | non-fusion elementwise | flops 262144 | bytes 1572864 | tf_op jit(solution)/shard_map/convert_element_type | solution.py:40
  9.4 0.0 all-gather.2.cloned.1.call-update
  9.4 0.0 reduce-scatter.5.cloned.1.call-start
  9.4 0.0 copy-done.1
  9.5 3.0 %collective-permute-start = (bf16[32,1024]{1,0:T(8,128)(2,1)S(1)}, bf16[32,1024]{1,0:T(8,128)(2,1)S(1)}, u32[]{:S(2)}, u32[]{:S(2)}) collective-permute-start(bf16[32,1024]{1,0:T(8,128)(2,1)S(1)} %get-tuple-element.10), channel_id=1, source_target_pairs={{0,2},{2,4},{4,6},{6,8},{8,10},{10,12},{12,14},{14,0},{1,3},{3,5},... | collective-permute-start | bytes 196616 | tf_op jit(solution)/shard_map/ppermute | solution.py:21
  12.5 0.0 copy-done.3
  12.5 0.0 copy-done.2
  12.6 5.2 %collective-permute-done = bf16[32,1024]{1,0:T(8,128)(2,1)S(1)} collective-permute-done((bf16[32,1024]{1,0:T(8,128)(2,1)S(1)}, bf16[32,1024]{1,0:T(8,128)(2,1)S(1)}, u32[]{:S(2)}, u32[]{:S(2)}) %collective-permute-start) | collective-permute-done | bytes 65568 | tf_op jit(solution)/shard_map/ppermute | solution.py:21
  17.7 0.0 collective-permute-start.1
  17.7 7.0 %collective-permute-done.1 = bf16[32,1024]{1,0:T(8,128)(2,1)S(1)} collective-permute-done((bf16[32,1024]{1,0:T(8,128)(2,1)S(1)}, bf16[32,1024]{1,0:T(8,128)(2,1)S(1)}, u32[]{:S(2)}, u32[]{:S(2)}) %collective-permute-start.1) | collective-permute-done | bytes 65568 | tf_op jit(solution)/shard_map/ppermute | solution.py:21
  24.7 0.0 collective-permute-start.2
  24.7 7.0 %collective-permute-done.2 = bf16[32,1024]{1,0:T(8,128)(2,1)S(1)} collective-permute-done((bf16[32,1024]{1,0:T(8,128)(2,1)S(1)}, bf16[32,1024]{1,0:T(8,128)(2,1)S(1)}, u32[]{:S(2)}, u32[]{:S(2)}) %collective-permute-start.2) | collective-permute-done | bytes 65568 | tf_op jit(solution)/shard_map/ppermute | solution.py:21
  31.7 0.0 collective-permute-start.3
  31.7 7.0 %collective-permute-done.3 = bf16[32,1024]{1,0:T(8,128)(2,1)S(1)} collective-permute-done((bf16[32,1024]{1,0:T(8,128)(2,1)S(1)}, bf16[32,1024]{1,0:T(8,128)(2,1)S(1)}, u32[]{:S(2)}, u32[]{:S(2)}) %collective-permute-start.3) | collective-permute-done | bytes 65568 | tf_op jit(solution)/shard_map/ppermute | solution.py:21
  38.6 0.0 collective-permute-start.4
  38.6 0.0 copy-start.4
  38.6 7.4 %collective-permute-done.4 = bf16[32,1024]{1,0:T(8,128)(2,1)S(1)} collective-permute-done((bf16[32,1024]{1,0:T(8,128)(2,1)S(1)}, bf16[32,1024]{1,0:T(8,128)(2,1)S(1)}, u32[]{:S(2)}, u32[]{:S(2)}) %collective-permute-start.4) | collective-permute-done | bytes 65568 | tf_op jit(solution)/shard_map/ppermute | solution.py:21
  46.0 0.0 collective-permute-start.5
  46.0 7.0 %collective-permute-done.5 = bf16[32,1024]{1,0:T(8,128)(2,1)S(1)} collective-permute-done((bf16[32,1024]{1,0:T(8,128)(2,1)S(1)}, bf16[32,1024]{1,0:T(8,128)(2,1)S(1)}, u32[]{:S(2)}, u32[]{:S(2)}) %collective-permute-start.5) | collective-permute-done | bytes 65568 | tf_op jit(solution)/shard_map/ppermute | solution.py:21
  53.0 0.0 collective-permute-start.6
  53.0 7.0 %collective-permute-done.6 = bf16[32,1024]{1,0:T(8,128)(2,1)S(1)} collective-permute-done((bf16[32,1024]{1,0:T(8,128)(2,1)S(1)}, bf16[32,1024]{1,0:T(8,128)(2,1)S(1)}, u32[]{:S(2)}, u32[]{:S(2)}) %collective-permute-start.6) | collective-permute-done | bytes 65568 | tf_op jit(solution)/shard_map/ppermute | solution.py:21
  59.9 0.6 gather_fusion
  60.5 0.0 all-gather.2.cloned.1.call-done
  60.6 0.0 copy-start
  60.6 1.8 %fusion.21 = (f32[512]{0:T(512)S(1)}, f32[256,512]{1,0:T(8,128)S(1)}) fusion(bf16[256,1024]{1,0:T(8,128)(2,1)S(1)} %bitcast.61, bf16[512,1024]{1,0:T(8,128)(2,1)} %all-gather.2.cloned.1.call-done), kind=kOutput, calls=%fused_computation.46 | convolution fusion | flops 268697088 | bytes 2099200 | tf_op jit(solution)/shard_map/dot_general | solution.py:63
  62.4 2.5 %pmax.7 = f32[512]{0:T(512)S(1)} all-reduce(f32[512]{0:T(512)S(1)} %get-tuple-element.27), channel_id=1, replica_groups=mesh['groups'=2,'wide'=8,'narrow'=2] {'narrow'}, use_global_device_ids=true, to_apply=%region_1.2 | all-reduce | flops 512 | bytes 4096 | tf_op jit(solution)/shard_map/pmax | solution.py:79
  64.9 1.1 fusion.2
  65.9 2.5 %all-reduce = (f32[512]{0:T(512)S(1)}, f32[512]{0:T(512)S(1)}) all-reduce(f32[512]{0:T(512)S(1)} %exponential_multiply_fusion, f32[512]{0:T(512)S(1)} %get-tuple-element.3), channel_id=1, replica_groups=mesh['groups'=2,'wide'=8,'narrow'=2] {'narrow'}, use_global_device_ids=true, to_apply=%region_3.4 | all-reduce | flops 1024 | bytes 8192 | tf_op jit(solution)/shard_map/psum | solution.py:80
  68.4 0.6 divide_subtract_fusion
  69.0 0.0 copy-done.4
  69.0 0.0 copy-done
  69.0 2.3 %fusion.16 = f32[256,1024]{1,0:T(8,128)} fusion(bf16[512,1024]{1,0:T(8,128)(2,1)S(1)} %copy-done, f32[256,512]{1,0:T(8,128)S(1)} %get-tuple-element.28, f32[512]{0:T(512)S(1)} %convert_element_type.94, f32[512]{0:T(512)S(1)} %get-tuple-element.8, f32[512]{0:T(512)S(1)} %copy-done.4, s32[512]{0:T(512)S(1)} %bitcast.106, s32[512]{0:T(512)S(1)} %bitcast.109, ...), kind=kOutput, calls=%fused_computation.43 | convolution fusion | flops 275382272 | bytes 2661376 | tf_op jit(solution)/shard_map/dot_general | solution.py:100
  71.3 0.0 reduce-scatter.5.cloned.1.call-update
  71.3 0.0 reduce-scatter.3.cloned.1.call-start
  71.4 2.7 %fusion.18 = f32[512,1024]{1,0:T(8,128)} fusion(bf16[256,1024]{1,0:T(8,128)(2,1)S(1)} %bitcast.62, f32[256,512]{1,0:T(8,128)S(1)} %get-tuple-element.28, f32[512]{0:T(512)S(1)} %convert_element_type.94, f32[512]{0:T(512)S(1)} %get-tuple-element.8, f32[512]{0:T(512)S(1)} %copy-done.4, s32[512]{0:T(512)S(1)} %bitcast.107, s32[512]{0:T(512)S(1)} %bitcast.110, ...), kind=kOutput, calls=%fused_computation.44 | convolution fusion | flops 275382272 | bytes 3185664 | tf_op jit(solution)/shard_map/dot_general | solution.py:93
  74.1 0.0 reduce-scatter.3.cloned.1.call-update
  74.1 58.3 %reduce-scatter.5.cloned.1.call-done = f32[32,1024]{1,0:T(8,128)} async-done(((f32[256,1024]{1,0:T(8,128)}), f32[32,1024]{1,0:T(8,128)}) %reduce-scatter.5.cloned.1.call-update) | async-done | bytes 131088 | tf_op jit(solution)/shard_map/reduce_scatter | solution.py:99
  132.4 11.6 %reduce-scatter.3.cloned.1.call-done = f32[256,1024]{1,0:T(8,128)} async-done(((f32[512,1024]{1,0:T(8,128)}), f32[256,1024]{1,0:T(8,128)}) %reduce-scatter.3.cloned.1.call-update) | async-done | bytes 1048592 | tf_op jit(solution)/shard_map/reduce_scatter | solution.py:98
  (14 shorter events, 0.1 us)
Async XLA Ops:
  7.2 2.3 %copy-start.1 = (f32[32,1024]{1,0:T(8,128)S(1)}, f32[32,1024]{1,0:T(8,128)}, u32[]{:S(2)}) copy-start(f32[32,1024]{1,0:T(8,128)} %param.6) | copy-start | bytes 393220
  7.2 5.3 %copy-start.3 = (s32[512]{0:T(512)S(1)}, s32[512]{0:T(512)}, u32[]{:S(2)}) copy-start(s32[512]{0:T(512)} %param.7) | copy-start | bytes 6148
  7.2 5.3 %copy-start.2 = (s32[512,16]{0,1:T(8,128)S(1)}, s32[512,16]{0,1:T(8,128)}, u32[]{:S(2)}) copy-start(s32[512,16]{0,1:T(8,128)} %param.8) | copy-start | bytes 98308
  7.2 53.4 %all-gather.2.cloned.1.call-start = ((), (), s32[]{:S(2)}) async-start(), calls=%async_computation.2 | async-start | bytes 1572864 | tf_op jit(solution)/shard_map/all_gather | solution.py:48
  9.4 123.1 %reduce-scatter.5.cloned.1.call-start = ((), (), s32[]{:S(2)}) async-start(), calls=%async_computation.4 | async-start | bytes 1179648 | tf_op jit(solution)/shard_map/reduce_scatter | solution.py:99
  9.5 8.3 %collective-permute-start = (bf16[32,1024]{1,0:T(8,128)(2,1)S(1)}, bf16[32,1024]{1,0:T(8,128)(2,1)S(1)}, u32[]{:S(2)}, u32[]{:S(2)}) collective-permute-start(bf16[32,1024]{1,0:T(8,128)(2,1)S(1)} %get-tuple-element.10), channel_id=1, source_target_pairs={{0,2},{2,4},{4,6},{6,8},{8,10},{10,12},{12,14},{14,0},{1,3},{3,5},... | collective-permute-start | bytes 196616 | tf_op jit(solution)/shard_map/ppermute | solution.py:21
  17.7 7.0 %collective-permute-start.1 = (bf16[32,1024]{1,0:T(8,128)(2,1)S(1)}, bf16[32,1024]{1,0:T(8,128)(2,1)S(1)}, u32[]{:S(2)}, u32[]{:S(2)}) collective-permute-start(bf16[32,1024]{1,0:T(8,128)(2,1)S(1)} %collective-permute-done), channel_id=1, source_target_pairs={{0,2},{2,4},{4,6},{6,8},{8,10},{10,12},{12,14},{14,0},{1,3},{3,5},... | collective-permute-start | bytes 196616 | tf_op jit(solution)/shard_map/ppermute | solution.py:21
  24.7 7.0 %collective-permute-start.2 = (bf16[32,1024]{1,0:T(8,128)(2,1)S(1)}, bf16[32,1024]{1,0:T(8,128)(2,1)S(1)}, u32[]{:S(2)}, u32[]{:S(2)}) collective-permute-start(bf16[32,1024]{1,0:T(8,128)(2,1)S(1)} %collective-permute-done.1), channel_id=1, source_target_pairs={{0,2},{2,4},{4,6},{6,8},{8,10},{10,12},{12,14},{14,0},{1,3},{3,5},... | collective-permute-start | bytes 196616 | tf_op jit(solution)/shard_map/ppermute | solution.py:21
  31.7 7.0 %collective-permute-start.3 = (bf16[32,1024]{1,0:T(8,128)(2,1)S(1)}, bf16[32,1024]{1,0:T(8,128)(2,1)S(1)}, u32[]{:S(2)}, u32[]{:S(2)}) collective-permute-start(bf16[32,1024]{1,0:T(8,128)(2,1)S(1)} %collective-permute-done.2), channel_id=1, source_target_pairs={{0,2},{2,4},{4,6},{6,8},{8,10},{10,12},{12,14},{14,0},{1,3},{3,5},... | collective-permute-start | bytes 196616 | tf_op jit(solution)/shard_map/ppermute | solution.py:21
  38.6 7.4 %collective-permute-start.4 = (bf16[32,1024]{1,0:T(8,128)(2,1)S(1)}, bf16[32,1024]{1,0:T(8,128)(2,1)S(1)}, u32[]{:S(2)}, u32[]{:S(2)}) collective-permute-start(bf16[32,1024]{1,0:T(8,128)(2,1)S(1)} %collective-permute-done.3), channel_id=1, source_target_pairs={{0,2},{2,4},{4,6},{6,8},{8,10},{10,12},{12,14},{14,0},{1,3},{3,5},... | collective-permute-start | bytes 196616 | tf_op jit(solution)/shard_map/ppermute | solution.py:21
  38.6 30.4 %copy-start.4 = (f32[512]{0:T(512)S(1)}, f32[512]{0:T(512)}, u32[]{:S(2)}) copy-start(f32[512]{0:T(512)} %param.9) | copy-start | bytes 6148
  46.0 7.0 %collective-permute-start.5 = (bf16[32,1024]{1,0:T(8,128)(2,1)S(1)}, bf16[32,1024]{1,0:T(8,128)(2,1)S(1)}, u32[]{:S(2)}, u32[]{:S(2)}) collective-permute-start(bf16[32,1024]{1,0:T(8,128)(2,1)S(1)} %collective-permute-done.4), channel_id=1, source_target_pairs={{0,2},{2,4},{4,6},{6,8},{8,10},{10,12},{12,14},{14,0},{1,3},{3,5},... | collective-permute-start | bytes 196616 | tf_op jit(solution)/shard_map/ppermute | solution.py:21
  53.0 7.0 %collective-permute-start.6 = (bf16[32,1024]{1,0:T(8,128)(2,1)S(1)}, bf16[32,1024]{1,0:T(8,128)(2,1)S(1)}, u32[]{:S(2)}, u32[]{:S(2)}) collective-permute-start(bf16[32,1024]{1,0:T(8,128)(2,1)S(1)} %collective-permute-done.5), channel_id=1, source_target_pairs={{0,2},{2,4},{4,6},{6,8},{8,10},{10,12},{12,14},{14,0},{1,3},{3,5},... | collective-permute-start | bytes 196616 | tf_op jit(solution)/shard_map/ppermute | solution.py:21
  60.6 8.4 %copy-start = (bf16[512,1024]{1,0:T(8,128)(2,1)S(1)}, bf16[512,1024]{1,0:T(8,128)(2,1)}, u32[]{:S(2)}) copy-start(bf16[512,1024]{1,0:T(8,128)(2,1)} %all-gather.2.cloned.1.call-done) | copy-start | bytes 3145732
  71.3 72.7 %reduce-scatter.3.cloned.1.call-start = ((), (), s32[]{:S(2)}) async-start(), calls=%async_computation.3 | async-start | bytes 3145728 | tf_op jit(solution)/shard_map/reduce_scatter | solution.py:98
Sparse Core Ops, SparseCore 0:
  10.1 11.7 all-gather.1
  71.4 60.9 reduce-scatter.4
  135.3 8.6 reduce-scatter.2
